TPU v7x, 32 devices: a whole 2x2x4 slice. The times are simulated.
32 devices in a mesh: wide: 8 (over z, y), narrow: 4 (over x, core).
Axes of the slice: x: 2, y: 2, z: 4, core: 2. Of those that a mesh axis runs over, the one named last changes fastest.
Arguments:
- tokens: bfloat16 [32768, 768], P(('wide', 'narrow')), may hold values from -6 to 6
- segment_ids: int32 [32768], P(('wide', 'narrow')), may hold values from 0 to 4, as said below
- cotangent: bfloat16 [32768, 768], P(('wide', 'narrow')), may hold values from -6 to 6
- ln1_gain: bfloat16 [768], P('wide'), may hold values from 0.5 to 1.5
- ln1_bias: bfloat16 [768], P('wide'), may hold values from -1 to 1
- qkv_weight: bfloat16 [768, 2304], P('wide'), may hold values from -0.3125 to 0.3125
- qv_bias: bfloat16 [1536], P('wide'), may hold values from -1 to 1
- out_weight: bfloat16 [768, 768], P('wide'), may hold values from -0.625 to 0.625
- out_bias: bfloat16 [768], P('wide'), may hold values from -1 to 1
- ln2_gain: bfloat16 [768], P('wide'), may hold values from 0.5 to 1.5
- ln2_bias: bfloat16 [768], P('wide'), may hold values from -1 to 1
- up_weight: bfloat16 [768, 3072], P('wide'), may hold values from -0.21875 to 0.21875
- up_bias: bfloat16 [3072], P('wide'), may hold values from -1 to 1
- down_weight: bfloat16 [3072, 768], P('wide'), may hold values from -0.109375 to 0.109375
- down_bias: bfloat16 [768], P('wide'), may hold values from -1 to 1
Outputs:
- output: bfloat16 [32768, 768], P(('wide', 'narrow'))
- tokens_grad: float32 [32768, 768], P(('wide', 'narrow'))
- ln1_gain_grad: float32 [768], P('wide')
- ln1_bias_grad: float32 [768], P('wide')
- qkv_weight_grad: float32 [768, 2304], P('wide')
- qv_bias_grad: float32 [1536], P('wide')
- out_weight_grad: float32 [768, 768], P('wide')
- out_bias_grad: float32 [768], P('wide')
- ln2_gain_grad: float32 [768], P('wide')
- ln2_bias_grad: float32 [768], P('wide')
- up_weight_grad: float32 [768, 3072], P('wide')
- up_bias_grad: float32 [3072], P('wide')
- down_weight_grad: float32 [3072, 768], P('wide')
- down_bias_grad: float32 [768], P('wide')
Inputs may be any that keep to these rules, and one draw needn't show every extreme that they name: In each sequence of 1024 rows, segment_ids at position p is (offset + p) // 256 for one offset of 1 to 255 of that sequence.
All inputs are finite; a program needn't handle non-finite values.
Results may differ from a plain program's by a relative error of at most 0.017.
Values may be sent and summed in bfloat16 or wider, within the bound.
No kernel may reach another device: no remote copies, remote signals or barrier semaphores. Data moves between devices by JAX's collectives and lax.ppermute only.
A program may use at most 192 MiB of HBM per device.

v0:
```python
from functools import partial

import jax
import jax.numpy as jnp
from jax import lax
from jax.sharding import PartitionSpec as P

D = 768
HEADS = 16
HEAD_DIM = 48
LENGTH = 1024
HGROUP = 4
BLOCK = 512


EPSILON = 1e-06
NEGATIVE = -1e30


def normalized_rows(value, gain, shift):
    centred = value - jnp.mean(value, axis=-1, keepdims=True)
    inverse = lax.rsqrt(jnp.mean(centred * centred, axis=-1, keepdims=True) + EPSILON)
    normed = centred * inverse
    return (normed * gain + shift, normed, inverse)


def norm_back(upper, normed, inverse, gain):
    scaled = upper * gain
    return inverse * (
        scaled
        - jnp.mean(scaled, axis=-1, keepdims=True)
        - normed * jnp.mean(scaled * normed, axis=-1, keepdims=True)
    )


def column_sum(value):
    return jnp.sum(value.astype(jnp.float32), axis=0)


def product(left, right):
    return jnp.dot(left, right, preferred_element_type=jnp.float32)


def left_product(left, right):
    return lax.dot_general(
        left, right, (((0,), (0,)), ((), ())), preferred_element_type=jnp.float32
    )


def right_product(left, right):
    return lax.dot_general(
        left, right, (((1,), (1,)), ((), ())), preferred_element_type=jnp.float32
    )


def to_groups(packed):
    seq_count = packed.shape[0] // LENGTH
    layers = packed.shape[1] // D
    shaped = packed.reshape(seq_count, LENGTH, layers, HEADS // HGROUP, HGROUP, HEAD_DIM)
    shaped = jnp.transpose(shaped, (0, 3, 2, 4, 1, 5))
    return shaped.reshape(seq_count * (HEADS // HGROUP), layers, HGROUP, LENGTH, HEAD_DIM)


def from_groups(grouped):
    seq_count = grouped.shape[0] // (HEADS // HGROUP)
    layers = grouped.shape[1]
    shaped = grouped.reshape(seq_count, HEADS // HGROUP, layers, HGROUP, LENGTH, HEAD_DIM)
    shaped = jnp.transpose(shaped, (0, 4, 2, 1, 3, 5))
    return shaped.reshape(seq_count * LENGTH, layers * D)


def block_scores(queries, keys, row_ids, key_ids):
    scores = jnp.einsum(
        "hqd,hkd->hqk", queries, keys, preferred_element_type=jnp.float32
    ) * HEAD_DIM ** (-0.5)
    same = row_ids[:, None] == key_ids[None, :]
    return jnp.where(same[None], scores, NEGATIVE)


def attend_forward(item):
    packed, segments = item
    queries, keys, values = (packed[0], packed[1], packed[2])
    results = []
    logsums = []
    for begin in range(0, LENGTH, BLOCK):
        scores = block_scores(
            queries[:, begin : begin + BLOCK], keys, segments[begin : begin + BLOCK], segments
        )
        highest = jnp.max(scores, axis=-1, keepdims=True)
        expo = jnp.exp(scores - highest)
        totals = jnp.sum(expo, axis=-1, keepdims=True)
        weights = (expo / totals).astype(jnp.bfloat16)
        results.append(
            jnp.einsum("hqk,hkd->hqd", weights, values, preferred_element_type=jnp.float32).astype(
                jnp.bfloat16
            )
        )
        logsums.append((highest + jnp.log(totals))[..., 0])
    return (jnp.concatenate(results, axis=1)[None], jnp.concatenate(logsums, axis=1))


def attend_backward(item):
    packed, segments, logsums, upper = item
    queries, keys, values = (packed[0], packed[1], packed[2])
    upper = upper[0]
    scale = HEAD_DIM ** (-0.5)
    key_grad = jnp.zeros(keys.shape, jnp.float32)
    value_grad = jnp.zeros(values.shape, jnp.float32)
    query_parts = []
    for begin in range(0, LENGTH, BLOCK):
        block_queries = queries[:, begin : begin + BLOCK]
        scores = block_scores(block_queries, keys, segments[begin : begin + BLOCK], segments)
        probs = jnp.exp(scores - logsums[:, begin : begin + BLOCK, None])
        block_upper = upper[:, begin : begin + BLOCK]
        prob_grad = jnp.einsum(
            "hqd,hkd->hqk", block_upper, values, preferred_element_type=jnp.float32
        )
        centre = jnp.sum(probs * prob_grad, axis=-1, keepdims=True)
        score_grad = (probs * (prob_grad - centre)).astype(jnp.bfloat16)
        value_grad = value_grad + jnp.einsum(
            "hqk,hqd->hkd",
            probs.astype(jnp.bfloat16),
            block_upper,
            preferred_element_type=jnp.float32,
        )
        query_parts.append(
            jnp.einsum("hqk,hkd->hqd", score_grad, keys, preferred_element_type=jnp.float32) * scale
        )
        key_grad = (
            key_grad
            + jnp.einsum(
                "hqk,hqd->hkd", score_grad, block_queries, preferred_element_type=jnp.float32
            )
            * scale
        )
    return jnp.stack([jnp.concatenate(query_parts, axis=1), key_grad, value_grad]).astype(
        jnp.bfloat16
    )


def shards(
    tokens,
    segment_ids,
    cotangent,
    ln1_gain,
    ln1_bias,
    qkv_weight,
    qv_bias,
    out_weight,
    out_bias,
    ln2_gain,
    ln2_bias,
    up_weight,
    up_bias,
    down_weight,
    down_bias,
):
    gain_one, shift_one, mix_weight, mix_bias, proj_weight, proj_bias = (
        lax.all_gather(ln1_gain, "wide", axis=0, tiled=True),
        lax.all_gather(ln1_bias, "wide", axis=0, tiled=True),
        lax.all_gather(qkv_weight, "wide", axis=0, tiled=True),
        lax.all_gather(qv_bias, "wide", axis=0, tiled=True),
        lax.all_gather(out_weight, "wide", axis=0, tiled=True),
        lax.all_gather(out_bias, "wide", axis=0, tiled=True),
    )
    inputs = tokens.astype(jnp.float32)
    seq_count = tokens.shape[0] // LENGTH
    groups = HEADS // HGROUP
    first_normalized, first_standardized, first_inverse_deviation = normalized_rows(
        inputs, gain_one.astype(jnp.float32), shift_one.astype(jnp.float32)
    )
    first_normalized = first_normalized.astype(jnp.bfloat16)
    mix_float = mix_bias.astype(jnp.float32)
    bias_all = jnp.concatenate([mix_float[:D], jnp.zeros((D,), jnp.float32), mix_float[D:]])
    qkv = (product(first_normalized, mix_weight) + bias_all).astype(jnp.bfloat16)
    packed = to_groups(qkv)
    item_ids = jnp.broadcast_to(
        segment_ids.reshape(seq_count, 1, LENGTH), (seq_count, groups, LENGTH)
    ).reshape(seq_count * groups, LENGTH)
    grouped_out, logsums = lax.map(attend_forward, (packed, item_ids))
    attended = from_groups(grouped_out)
    after = inputs + product(attended, proj_weight) + proj_bias.astype(jnp.float32)
    gain_two, shift_two, up_full, up_shift, down_full, down_shift = (
        lax.all_gather(ln2_gain, "wide", axis=0, tiled=True),
        lax.all_gather(ln2_bias, "wide", axis=0, tiled=True),
        lax.all_gather(up_weight, "wide", axis=0, tiled=True),
        lax.all_gather(up_bias, "wide", axis=0, tiled=True),
        lax.all_gather(down_weight, "wide", axis=0, tiled=True),
        lax.all_gather(down_bias, "wide", axis=0, tiled=True),
    )
    second_normalized, second_standardized, second_inverse_deviation = normalized_rows(
        after, gain_two.astype(jnp.float32), shift_two.astype(jnp.float32)
    )
    second_normalized = second_normalized.astype(jnp.bfloat16)
    pre = product(second_normalized, up_full) + up_shift.astype(jnp.float32)
    hidden, gelu_pull = jax.vjp(partial(jax.nn.gelu, approximate=False), pre)
    hidden = hidden.astype(jnp.bfloat16)
    output = (after + product(hidden, down_full) + down_shift.astype(jnp.float32)).astype(
        jnp.bfloat16
    )
    second_gain_backward, back_up, back_down = (
        lax.all_gather(ln2_gain, "wide", axis=0, tiled=True),
        lax.all_gather(up_weight, "wide", axis=0, tiled=True),
        lax.all_gather(down_weight, "wide", axis=0, tiled=True),
    )
    upstream = cotangent.astype(jnp.float32)
    down_bias_part = column_sum(cotangent)
    down_weight_part = left_product(hidden, cotangent)
    hidden_grad = right_product(cotangent, back_down)
    pre_grad = gelu_pull(hidden_grad)[0].astype(jnp.bfloat16)
    up_bias_part = column_sum(pre_grad)
    up_weight_part = left_product(second_normalized, pre_grad)
    second_normalized_grad = right_product(pre_grad, back_up)
    second_gain_shard = jnp.sum(second_normalized_grad * second_standardized, axis=0)
    shift_two_part = jnp.sum(second_normalized_grad, axis=0)
    after_grad = upstream + norm_back(
        second_normalized_grad,
        second_standardized,
        second_inverse_deviation,
        second_gain_backward.astype(jnp.float32),
    )
    wide_gain_two, wide_shift_two, wide_up, wide_up_bias, wide_down, wide_down_bias = (
        lax.psum_scatter(second_gain_shard, "wide", scatter_dimension=0, tiled=True),
        lax.psum_scatter(shift_two_part, "wide", scatter_dimension=0, tiled=True),
        lax.psum_scatter(up_weight_part, "wide", scatter_dimension=0, tiled=True),
        lax.psum_scatter(up_bias_part, "wide", scatter_dimension=0, tiled=True),
        lax.psum_scatter(down_weight_part, "wide", scatter_dimension=0, tiled=True),
        lax.psum_scatter(down_bias_part, "wide", scatter_dimension=0, tiled=True),
    )
    first_gain_backward, back_mix, back_proj = (
        lax.all_gather(ln1_gain, "wide", axis=0, tiled=True),
        lax.all_gather(qkv_weight, "wide", axis=0, tiled=True),
        lax.all_gather(out_weight, "wide", axis=0, tiled=True),
    )
    proj_grad = after_grad.astype(jnp.bfloat16)
    proj_bias_part = column_sum(proj_grad)
    proj_weight_part = left_product(attended, proj_grad)
    attended_grad = right_product(proj_grad, back_proj).astype(jnp.bfloat16)
    grouped_upper = to_groups(attended_grad)
    grouped_grad = lax.map(attend_backward, (packed, item_ids, logsums, grouped_upper))
    qkv_grad = from_groups(grouped_grad)
    qkv_sums = column_sum(qkv_grad)
    mix_bias_part = jnp.concatenate([qkv_sums[:D], qkv_sums[2 * D :]])
    mix_weight_part = left_product(first_normalized, qkv_grad)
    first_normalized_grad = right_product(qkv_grad, back_mix)
    first_gain_shard = jnp.sum(first_normalized_grad * first_standardized, axis=0)
    shift_one_part = jnp.sum(first_normalized_grad, axis=0)
    tokens_grad = after_grad + norm_back(
        first_normalized_grad,
        first_standardized,
        first_inverse_deviation,
        first_gain_backward.astype(jnp.float32),
    )
    wide_gain_one, wide_shift_one, wide_mix, wide_mix_bias, wide_proj, wide_proj_bias = (
        lax.psum_scatter(first_gain_shard, "wide", scatter_dimension=0, tiled=True),
        lax.psum_scatter(shift_one_part, "wide", scatter_dimension=0, tiled=True),
        lax.psum_scatter(mix_weight_part, "wide", scatter_dimension=0, tiled=True),
        lax.psum_scatter(mix_bias_part, "wide", scatter_dimension=0, tiled=True),
        lax.psum_scatter(proj_weight_part, "wide", scatter_dimension=0, tiled=True),
        lax.psum_scatter(proj_bias_part, "wide", scatter_dimension=0, tiled=True),
    )
    summed = (
        lax.psum(wide_gain_one.astype(jnp.bfloat16), "narrow").astype(jnp.float32),
        lax.psum(wide_shift_one.astype(jnp.bfloat16), "narrow").astype(jnp.float32),
        lax.psum(wide_mix.astype(jnp.bfloat16), "narrow").astype(jnp.float32),
        lax.psum(wide_mix_bias.astype(jnp.bfloat16), "narrow").astype(jnp.float32),
        lax.psum(wide_proj.astype(jnp.bfloat16), "narrow").astype(jnp.float32),
        lax.psum(wide_proj_bias.astype(jnp.bfloat16), "narrow").astype(jnp.float32),
        lax.psum(wide_gain_two.astype(jnp.bfloat16), "narrow").astype(jnp.float32),
        lax.psum(wide_shift_two.astype(jnp.bfloat16), "narrow").astype(jnp.float32),
        lax.psum(wide_up.astype(jnp.bfloat16), "narrow").astype(jnp.float32),
        lax.psum(wide_up_bias.astype(jnp.bfloat16), "narrow").astype(jnp.float32),
        lax.psum(wide_down.astype(jnp.bfloat16), "narrow").astype(jnp.float32),
        lax.psum(wide_down_bias.astype(jnp.bfloat16), "narrow").astype(jnp.float32),
    )
    return (
        output,
        tokens_grad,
        summed[0],
        summed[1],
        summed[2],
        summed[3],
        summed[4],
        summed[5],
        summed[6],
        summed[7],
        summed[8],
        summed[9],
        summed[10],
        summed[11],
    )


def solution(mesh):
    placed = (
        P(("wide", "narrow"), None),
        P(("wide", "narrow")),
        P(("wide", "narrow"), None),
        P("wide"),
        P("wide"),
        P("wide", None),
        P("wide"),
        P("wide", None),
        P("wide"),
        P("wide"),
        P("wide"),
        P("wide", None),
        P("wide"),
        P("wide", None),
        P("wide"),
    )
    return jax.shard_map(
        shards,
        mesh=mesh,
        in_specs=placed,
        out_specs=(
            P(("wide", "narrow"), None),
            P(("wide", "narrow"), None),
            P("wide"),
            P("wide"),
            P("wide", None),
            P("wide"),
            P("wide", None),
            P("wide"),
            P("wide"),
            P("wide"),
            P("wide", None),
            P("wide"),
            P("wide", None),
            P("wide"),
        ),
        check_vma=False,
    )
```

profile of v0, /device:TPU:0, one launch (start us, length us, event | category | flops | bytes accessed | tf_op | source)
XLA Modules:
  0.0 1006.8 jit_solution(17391298173697885210)
XLA Ops:
  19.2 40.7 %all-reduce.16 = (bf16[1536]{0:T(1024)(128)(2,1)S(1)}, bf16[768]{0:T(1024)(128)(2,1)S(1)}, bf16[768]{0:T(1024)(128)(2,1)S(1)}, bf16[768]{0:T(1024)(128)(2,1)S(1)...) all-reduce(bf16[1536]{0:T(1024)(128)(2,1)S(1)} %dynamic-update-slic, ...), channel_id=1, replica_groups=mesh['wide'=8,'narrow'=4] {'wide'}, use_global_device_ids=true, to_apply=%add.2 | all-reduce | flops 6144 | bytes 24576
  61.7 26.4 %all-gather = bf16[8,1,384]{2,1,0:T(2,128)(2,1)S(1)} all-gather(bf16[1,1,384]{2,1,0:T(2,128)(2,1)S(1)} %reshape.346), channel_id=1, replica_groups=mesh['wide'=8,'narrow'=4] {'wide'}, dimensions={0}, use_global_device_ids=true | all-gather | bytes 6912 | tf_op jit(solution)/shard_map/all_gather | solution.py:187
  92.9 7.8 add_convert_fusion.1
  100.7 6.6 copy.53
  107.4 5.3 copy.54
  112.7 82.5 %while.22 = (s32[]{:T(128)}, bf16[4,1,4,1024,48]{3,4,2,1,0:T(8,128)(2,1)}, f32[4,4,1024]{2,1,0:T(4,128)S(1)}, s32[4,1024]{1,0:T(4,128)S(1)}, bf16[4,3,4,1024,48]...) while((s32[]{:T(128)}, bf16[4,1,4,1024,48]{3,4,2,1,0:T(8,128)(2,1)}, ...), condition=%wide.region_7.8_spmd, body=%wide.region_2.7_spmd.sunk | while | flops 857669632 | bytes 58646728 | solution.py:180
  120.6 4.7 fusion.159
  129.0 3.8 fusion.160
  141.1 4.7 fusion.159
  149.6 3.8 fusion.160
  161.7 4.7 fusion.159
  166.4 3.8 fusion.161
  170.1 3.8 fusion.160
  182.2 4.7 fusion.159
  186.9 3.8 fusion.161
  190.7 3.8 fusion.160
  195.3 5.0 fusion.102
  202.7 50.5 %multiply_convert_fusion.2 = (bf16[1024,3072]{1,0:T(8,128)(2,1)}, f32[1024,3072]{1,0:T(8,128)}, f32[1024,3072]{1,0:T(8,128)}) fusion(f32[3072]{0:T(1024)S(1)} %bitcast.173, bf16[768,3072]{1,0:T(8,128)(2,1)} %all-gather.10.cloned.1.call-done, f32[1024,768]{0,1:T(8,128)} %get-tuple-element.230, f32[768]{0:T(1024)S(1)} %copy-done.25, f32[768]{0:T(1024)S(1)} %copy-done.15, ...), kind=kOutput, calls=%fused_computation.101 | convolution fusion | flops 5043388416 | bytes 39348224 | tf_op jit(solution)/shard_map/dot_general | solution.py:41
  253.2 27.2 %all-gather.12.cloned.1.call-done = bf16[3072,768]{1,0:T(8,128)(2,1)} async-done(((bf16[384,768]{1,0:T(8,128)(2,1)}), bf16[3072,768]{1,0:T(8,128)(2,1)}) %all-gather.12.cloned.1.call-update) | async-done | bytes 4718608 | tf_op jit(solution)/shard_map/all_gather | solution.py:188
  280.4 17.4 %convert_reduce_fusion = (f32[3072]{0:T(1024)}, bf16[1024,3072]{1,0:T(8,128)(2,1)}) fusion(f32[1024,3072]{1,0:T(8,128)} %get-tuple-element.199, bf16[1024,768]{1,0:T(8,128)(2,1)S(1)} %copy-done.6, bf16[3072,768]{1,0:T(8,128)(2,1)} %all-gather.12.cloned.1.call-done, f32[1024,3072]{1,0:T(8,128)} %get-tuple-element.231, f32[3072]{0:T(1024)S(1)} %bitcast.174), kind=kOutput, calls=%fused_computation.99 | convolution fusion | flops 4885312512 | bytes 37773312 | tf_op jit(solution)/shard_map/dot_general | solution.py:51
  297.8 10.3 %fusion.104 = (f32[768]{0:T(1024)}, f32[1024,768]{1,0:T(8,128)}) fusion(bf16[1024,3072]{1,0:T(8,128)(2,1)} %get-tuple-element.237, bf16[768,3072]{1,0:T(8,128)(2,1)} %all-gather.10.cloned.1.call-done), kind=kOutput, calls=%fused_computation.177 | convolution fusion | flops 4832623616 | bytes 14158848 | tf_op jit(solution)/shard_map/dot_general | solution.py:51
  314.1 4.4 convert_reduce_fusion.4
  323.1 4.4 convolution_convert_fusion
  327.6 147.7 %while.23 = (s32[]{:T(128)}, bf16[4,3,4,1024,48]{3,4,2,0,1:T(8,128)(2,1)}, s32[4,1024]{1,0:T(4,128)S(1)}, bf16[4,3,4,1024,48]{3,4,2,1,0:T(8,128)(2,1)}, f32[4,4,...) while((s32[]{:T(128)}, ...), condition=%wide.region_15.16_spmd, body=%wide.region_12.15_spmd.sunk | while | flops 2082926592 | bytes 143171824 | solution.py:240
  339.5 6.4 multiply_reduce_fusion.10
  345.9 4.7 multiply_convert_fusion.6
  353.0 4.2 multiply_reduce_fusion.9
  376.4 6.4 multiply_reduce_fusion.10
  382.7 4.7 multiply_convert_fusion.6
  389.8 4.2 multiply_reduce_fusion.9
  413.1 6.4 multiply_reduce_fusion.10
  419.5 4.7 multiply_convert_fusion.6
  426.5 4.2 multiply_reduce_fusion.9
  449.8 6.4 multiply_reduce_fusion.10
  456.2 4.7 multiply_convert_fusion.6
  463.3 4.2 multiply_reduce_fusion.9
  475.3 8.7 fusion.92
  484.7 10.6 %fusion.95 = f32[768,3072]{1,0:T(8,128)} fusion(bf16[1024,3072]{1,0:T(8,128)(2,1)} %get-tuple-element.237, f32[1024,768]{0,1:T(8,128)} %get-tuple-element.230, f32[768]{0:T(1024)S(1)} %copy-done.26, f32[768]{0:T(1024)S(1)} %copy-done.16, f32[1024]{0:T(1024)S(1)} %copy-done.18, f32[1024]{0:T(1024)S(1)} %copy-done.10), kind=kOutput, calls=%fused_computation.169 | convolution fusion | flops 4835770368 | bytes 18888704 | tf_op jit(solution)/shard_map/dot_general | solution.py:45
  495.3 9.9 fusion.105
  507.2 10.1 %add_convert_fusion.2 = bf16[1024,768]{0,1:T(8,128)(2,1)} fusion(f32[1024,768]{0,1:T(8,128)} %get-tuple-element.230, bf16[1024,3072]{1,0:T(8,128)(2,1)} %get-tuple-element.198, bf16[3072,768]{1,0:T(8,128)(2,1)} %all-gather.12.cloned.1.call-done, f32[768]{0:T(1024)S(1)} %convert_element_type.183), kind=kOutput, calls=%fused_computation.140 | convolution fusion | flops 4834197504 | bytes 15731712 | tf_op jit(solution)/shard_map/dot_general | solution.py:41
  523.3 9.0 fusion.103
  539.0 35.8 %all-reduce.15 = (bf16[768]{0:T(1024)(128)(2,1)S(1)}, bf16[768]{0:T(1024)(128)(2,1)S(1)}, bf16[1536]{0:T(1024)(128)(2,1)S(1)}, bf16[768]{0:T(1024)(128)(2,1)S(1)...) all-reduce(f32[768]{0:T(1024)S(1)} %get-tuple-element.143, ...), channel_id=2, replica_groups=mesh['wide'=8,'narrow'=4] {'wide'}, use_global_device_ids=true, to_apply=%region_19.20.clone | all-reduce | flops 9216 | bytes 55296
  575.4 5.7 all-reduce.17
  587.0 26.4 %reduce-scatter.5.cloned.1.call-done = f32[96,2304]{1,0:T(8,128)} async-done(((f32[768,2304]{1,0:T(8,128)}), f32[96,2304]{1,0:T(8,128)}) %reduce-scatter.5.cloned.1.call-update) | async-done | bytes 884752 | tf_op jit(solution)/shard_map/reduce_scatter | solution.py:257
  615.5 162.9 %reduce-scatter.9.cloned.1.call-done = f32[96,3072]{1,0:T(8,128)} async-done(((f32[768,3072]{1,0:T(8,128)}), f32[96,3072]{1,0:T(8,128)}) %reduce-scatter.9.cloned.1.call-update) | async-done | bytes 1179664 | tf_op jit(solution)/shard_map/reduce_scatter | solution.py:225
  780.5 162.7 %reduce-scatter.11.cloned.1.call-done = f32[384,768]{1,0:T(8,128)} async-done(((f32[3072,768]{1,0:T(8,128)}), f32[384,768]{1,0:T(8,128)}) %reduce-scatter.11.cloned.1.call-update) | async-done | bytes 1179664 | tf_op jit(solution)/shard_map/reduce_scatter | solution.py:227
  945.3 5.5 fusion.85
  954.5 37.6 %all-reduce.21.cloned.1.call-done = (bf16[96,2304]{1,0:T(8,128)(2,1)}, bf16[96,768]{1,0:T(8,128)(2,1)}, bf16[96,3072]{1,0:T(8,128)(2,1)}, bf16[384,768]{1,0:T(8,128)(2,1)}) async-done(((bf16[96,2304]{1,0:T(8,128)(2,1)}, bf16[96,768]{1,0:T(8,128)(2,1)}, bf16[96,3072]{1,0:T(8,128)(2,1)}, bf16[384,768]{1,0:T(8,128)(2,1)}), (bf16[96,2304]{1,0:T(8,128)(2,1)}, bf16[96,768]{1,0:T(8,128)(2,1)}, ...) | async-done | bytes 1769488 | tf_op jit(solution)/shard_map/psum | solution.py:265
  (278 shorter events, 194.2 us)
Async XLA Ops:
  7.2 84.1 %copy-start.5 = (bf16[1024,768]{1,0:T(8,128)(2,1)S(1)}, bf16[1024,768]{1,0:T(8,128)(2,1)}, u32[]{:S(2)}) copy-start(bf16[1024,768]{1,0:T(8,128)(2,1)} %param.21) | copy-start | bytes 4718596
  7.2 85.7 %all-gather.6.cloned.1.call-start = ((), (), s32[]{:S(2)}) async-start(), calls=%async_computation.4 | async-start | bytes 3981312 | tf_op jit(solution)/shard_map/all_gather | solution.py:161
  7.9 187.4 %all-gather.8.cloned.1.call-start = ((), (), s32[]{:S(2)}) async-start(), calls=%async_computation.5 | async-start | bytes 1327104 | tf_op jit(solution)/shard_map/all_gather | solution.py:163
  8.7 193.9 %all-gather.10.cloned.1.call-start = ((), (), s32[]{:S(2)}) async-start(), calls=%async_computation.6 | async-start | bytes 5308416 | tf_op jit(solution)/shard_map/all_gather | solution.py:186
  9.4 271.0 %all-gather.12.cloned.1.call-start = ((), (), s32[]{:S(2)}) async-start(), calls=%async_computation.7 | async-start | bytes 5308416 | tf_op jit(solution)/shard_map/all_gather | solution.py:188
  10.0 575.4 %reduce-scatter.7.cloned.1.call-start = ((), (), s32[]{:S(2)}) async-start(), calls=%async_computation.9 | async-start | bytes 2654208 | tf_op jit(solution)/shard_map/reduce_scatter | solution.py:259
  59.9 33.0 %copy-start.11 = (f32[768]{0:T(1024)}, f32[768]{0:T(1024)S(1)}, u32[]{:S(2)}) copy-start(f32[768]{0:T(1024)S(1)} %convert_element_type.172) | copy-start | bytes 9220
  60.5 32.4 %copy-start.27 = (f32[768]{0:T(1024)}, f32[768]{0:T(1024)S(1)}, u32[]{:S(2)}) copy-start(f32[768]{0:T(1024)S(1)} %convert_element_type.173) | copy-start | bytes 9220
  90.5 10.2 %copy-start = (bf16[1024,768]{0,1:T(8,128)(2,1)}, bf16[1024,768]{0,1:T(8,128)(2,1)S(1)}, u32[]{:S(2)}) copy-start(bf16[1024,768]{0,1:T(8,128)(2,1)S(1)} %copy.52) | copy-start | bytes 4718596
  90.8 10.0 copy-start.7
  91.2 9.5 copy-start.13
  107.4 5.4 copy-start.24
  112.7 82.6 %copy-start.1 = (bf16[1024,768]{0,1:T(8,128)(2,1)S(1)}, bf16[1024,768]{0,1:T(8,128)(2,1)}, u32[]{:S(2)}) copy-start(bf16[1024,768]{0,1:T(8,128)(2,1)} %copy-done) | copy-start | bytes 4718596
  112.7 82.6 %copy-start.29 = (f32[768]{0:T(1024)S(1)}, f32[768]{0:T(1024)}, u32[]{:S(2)}) copy-start(f32[768]{0:T(1024)} %convert_element_type.177) | copy-start | bytes 9220
  195.3 7.3 copy-start.15
  195.3 7.3 copy-start.22
  195.3 7.3 copy-start.25
  200.3 113.7 %copy-start.9 = (f32[1024]{0:T(1024)}, f32[1024]{0:T(1024)S(1)}, u32[]{:S(2)}) copy-start(f32[1024]{0:T(1024)S(1)} %broadcast_multiply_fusion.4) | copy-start | bytes 12292
  202.6 111.5 %copy-start.17 = (f32[1024]{0:T(1024)}, f32[1024]{0:T(1024)S(1)}, u32[]{:S(2)}) copy-start(f32[1024]{0:T(1024)S(1)} %add_rsqrt_fusion) | copy-start | bytes 12292
  202.6 77.7 %copy-start.6 = (bf16[1024,768]{1,0:T(8,128)(2,1)S(1)}, bf16[1024,768]{1,0:T(8,128)(2,1)}, u32[]{:S(2)}) copy-start(bf16[1024,768]{1,0:T(8,128)(2,1)} %param.21) | copy-start | bytes 4718596
  310.5 3.6 copy-start.4
  314.1 6.1 copy-start.32
  318.5 1.7 copy-start.3
  320.2 2.9 copy-start.33
  323.1 290.4 %reduce-scatter.5.cloned.1.call-start = ((), (), s32[]{:S(2)}) async-start(), calls=%async_computation.8 | async-start | bytes 7962624 | tf_op jit(solution)/shard_map/reduce_scatter | solution.py:257
  327.5 147.7 %copy-start.2 = (bf16[1024,768]{0,1:T(8,128)(2,1)S(1)}, bf16[1024,768]{0,1:T(8,128)(2,1)}, u32[]{:S(2)}) copy-start(bf16[1024,768]{0,1:T(8,128)(2,1)} %copy-done) | copy-start | bytes 4718596
  327.5 147.7 %copy-start.8 = (f32[1024]{0:T(1024)S(1)}, f32[1024]{0:T(1024)}, u32[]{:S(2)}) copy-start(f32[1024]{0:T(1024)} %copy-done.7) | copy-start | bytes 12292
  327.5 147.7 %copy-start.12 = (f32[768]{0:T(1024)S(1)}, f32[768]{0:T(1024)}, u32[]{:S(2)}) copy-start(f32[768]{0:T(1024)} %copy-done.11) | copy-start | bytes 9220
  327.5 147.7 %copy-start.14 = (f32[1024]{0:T(1024)S(1)}, f32[1024]{0:T(1024)}, u32[]{:S(2)}) copy-start(f32[1024]{0:T(1024)} %copy-done.13) | copy-start | bytes 12292
  327.6 147.7 %copy-start.28 = (f32[768]{0:T(1024)S(1)}, f32[768]{0:T(1024)}, u32[]{:S(2)}) copy-start(f32[768]{0:T(1024)} %copy-done.27) | copy-start | bytes 9220
  484.0 0.7 copy-start.10
  484.0 0.7 copy-start.16
  484.0 0.7 copy-start.18
  484.0 0.7 copy-start.26
  484.0 294.3 %reduce-scatter.9.cloned.1.call-start = ((), (), s32[]{:S(2)}) async-start(), calls=%async_computation.10 | async-start | bytes 10616832 | tf_op jit(solution)/shard_map/reduce_scatter | solution.py:225
  495.3 447.9 %reduce-scatter.11.cloned.1.call-start = ((), (), s32[]{:S(2)}) async-start(), calls=%async_computation.11 | async-start | bytes 10616832 | tf_op jit(solution)/shard_map/reduce_scatter | solution.py:227
  505.2 2.0 copy-start.31
  505.2 486.9 %all-reduce.21.cloned.1.call-start = ((), (), s32[]{:S(2)}) async-start(), calls=%async_computation.12 | async-start | bytes 3538944 | tf_op jit(solution)/shard_map/psum | solution.py:265
  532.4 6.6 copy-start.19
  532.4 6.6 copy-start.20
  532.4 6.6 copy-start.21
  532.4 6.6 copy-start.23
  532.4 6.6 copy-start.30
Sparse Core Ops, SparseCore 0:
  10.2 67.9 all-gather.5
  80.4 39.9 all-gather.7
  122.5 78.0 all-gather.9
  202.6 77.6 all-gather.11
  323.2 68.1 reduce-scatter.6
  484.1 129.3 reduce-scatter.4
  617.1 161.2 reduce-scatter.8
  781.9 161.1 reduce-scatter.10
  946.9 45.1 all-reduce.20
where the time goes:
time: 1020 us; the launch traced here: 1010 us
  waiting for transfers between devices  420 us (41%)
  matrix products  305 us (30%)
  blocking collectives  109 us (11%)
  other arithmetic  105 us (10%)
  local copies, waits for them, and re-layouts  48.5 us (5%)
  between operations  17.7 us (2%)
    reduce_scatter x1, waiting for transfers between devices, shards(): lax.psum_scatter(up_weight_part, 'wide', scatter_dimension=0, tiled=True)  163 us
    reduce_scatter x1, waiting for transfers between devices, shards(): lax.psum_scatter(down_weight_part, 'wide', scatter_dimension=0, tiled=True)  163 us
    unnamed x2, blocking collectives  76.5 us
    dot_general x4, matrix products, product(): return jnp.dot(left, right, preferred_element_type=jnp.float32)  73.4 us
    dot_general x8, matrix products, attend_backward(): jnp.einsum('hqd,hkd->hqk', block_upper, values, preferred_element_type=jn...  42.3 us
    dot_general x4, matrix products, right_product(): lax.dot_general(left, right, (((1,), (1,)), ((), ())), preferred_element_...  41.2 us
    dot_general x16, matrix products, block_scores(): jnp.einsum('hqd,hkd->hqk', queries, keys, preferred_element_type=jnp.floa...  41 us
    psum x1, waiting for transfers between devices, shards(): lax.psum(wide_mix.astype(jnp.bfloat16), 'narrow').astype(jnp.float32)  37.6 us
  transfers between devices with their start and end apart: 9, of which 5 were waited for; matrix products, arithmetic and copies ran while one was open for 40% of the time, Pallas kernels for 0%

commit v1 on v0

v1 whole, which is shorter than its diff:
```python
import functools
import jax
import jax.numpy as jnp
from jax import lax
from jax.experimental import pallas as pl
from jax.experimental.pallas import tpu as pltpu
from jax.sharding import PartitionSpec as P

D = 768
HEADS = 16
HEAD_DIM = 48
LENGTH = 1024
IMAGE = 256
TILES = LENGTH // IMAGE
EPSILON = 1e-06
LOG2E = 1.4426950408889634
SCALE2 = HEAD_DIM ** (-0.5) * LOG2E
f32 = jnp.float32
bf16 = jnp.bfloat16
FULL = pl.Buffered(1)
FF = 4 * D
SIZES = (("g1", D), ("b1", D), ("bq", 3 * D), ("bo", D), ("g2", D), ("b2", D), ("bu", FF), ("bd", D))
SPOTS = {}
TOTAL = 0
for NAME, SIZE in SIZES:
    SPOTS[NAME] = (TOTAL, SIZE)
    TOTAL += SIZE


def vec(ref, name, begin=0, size=None):
    at, full = SPOTS[name]
    return ref[:, at + begin:at + begin + (full if size is None else size)]


def whole(shape):
    return pl.BlockSpec(shape, lambda *_: (0,) * len(shape), pipeline_mode=FULL)


def rows(width):
    return pl.BlockSpec((IMAGE, width), lambda b, *_: (b, 0))


def kept(shape):
    return pl.BlockSpec(shape, lambda *_: (0,) * len(shape))


def dot(left, right, over):
    return lax.dot_general(left, right, ((over[0], over[1]), ((), ())), preferred_element_type=f32)


NN = ((1,), (0,))
NT = ((1,), (1,))
TN = ((0,), (0,))


def window(head):
    first = head * HEAD_DIM
    start = first // 128 * 128
    width = 128 if first + HEAD_DIM <= start + 128 else 256
    return first, start, width


def lane_mask(first, start, width):
    lane = lax.broadcasted_iota(jnp.int32, (1, width), 1) + start
    return (lane >= first) & (lane < first + HEAD_DIM)


def same_image(block, shift):
    size = IMAGE - shift
    row = lax.broadcasted_iota(jnp.int32, (IMAGE, 1), 0) < size
    col = lax.broadcasted_iota(jnp.int32, (1, IMAGE), 1) < size
    row = jnp.where(row, 1, 0)
    col = jnp.where(col, 1, 0)
    return (row == col) | (block < TILES - 1)


def standard(value):
    centred = value - jnp.mean(value, axis=-1, keepdims=True)
    inverse = lax.rsqrt(jnp.mean(centred * centred, axis=-1, keepdims=True) + EPSILON)
    return centred * inverse, inverse


def norm_back(upper, xhat, inverse, gain):
    scaled = upper * gain
    return inverse * (
        scaled
        - jnp.mean(scaled, axis=-1, keepdims=True)
        - xhat * jnp.mean(scaled * xhat, axis=-1, keepdims=True)
    )


def add_up(ref, value):
    @pl.when(pl.program_id(0) == 0)
    def _():
        ref[...] = jnp.zeros_like(ref)

    ref[...] += value


def col_sum(value):
    return jnp.sum(value, axis=0, keepdims=True)


def params(limit=56):
    return pltpu.CompilerParams(
        dimension_semantics=("arbitrary",), vmem_limit_bytes=limit * 1024 * 1024
    )


def aligned(shift):
    return pl.multiple_of(lax.shift_left(lax.shift_right_logical(shift, 3), 3), 8)


def taken(scratch, shift):
    near = scratch[pl.ds(aligned(shift), IMAGE + 8), :]
    back_by = (IMAGE + 8) - (shift - aligned(shift))
    return pltpu.roll(near, back_by, 0)[:IMAGE]


def attend_kernel(shift_ref, xa, xb, ca, cb, w, vecs,
                  x_out, c_out, n_out, qkv_out, att_out, lse_out, scratch):
    block = pl.program_id(0)
    shift = shift_ref[0]
    scratch[0:IMAGE] = ca[...].astype(f32)
    scratch[IMAGE:2 * IMAGE] = cb[...].astype(f32)
    c_out[...] = taken(scratch, shift).astype(bf16)
    scratch[0:IMAGE] = xa[...].astype(f32)
    scratch[IMAGE:2 * IMAGE] = xb[...].astype(f32)
    x = taken(scratch, shift)
    x_out[...] = x.astype(bf16)
    xhat, _ = standard(x)
    normed = (xhat * vec(vecs, "g1") + vec(vecs, "b1")).astype(bf16)
    n_out[...] = normed
    qkv_out[...] = (dot(normed, w[...], NN) + vec(vecs, "bq")).astype(bf16)
    same = same_image(block, shift)
    sums = [jnp.zeros((IMAGE, 128), f32) for _ in range(D // 128)]
    marks = jnp.zeros((IMAGE, 128), f32)
    lane = lax.broadcasted_iota(jnp.int32, (1, 128), 1)
    for head in range(HEADS):
        first, start, width = window(head)
        mask = lane_mask(first, start, width)
        q = qkv_out[:, start:start + width]
        k = qkv_out[:, D + start:D + start + width]
        v = qkv_out[:, 2 * D + start:2 * D + start + width]
        q = jnp.where(mask, q, jnp.zeros_like(q))
        v = jnp.where(mask, v, jnp.zeros_like(v))
        scores = jnp.where(same, dot(q, k, NT), -1e30)
        highest = jnp.max(scores, axis=-1, keepdims=True)
        expo = jnp.exp2((scores - highest) * SCALE2)
        total = jnp.sum(expo, axis=-1, keepdims=True)
        probs = (expo * (1.0 / total)).astype(bf16)
        part = dot(probs, v, NN)
        for t in range(width // 128):
            at = start // 128 + t
            sums[at] = sums[at] + part[:, 128 * t:128 * t + 128]
        marks = jnp.where(lane == head, highest * SCALE2 + jnp.log2(total), marks)
    for t in range(D // 128):
        att_out[:, 128 * t:128 * t + 128] = sums[t].astype(bf16)
    lse_out[...] = marks


def attend(shift, tokens, cot, w, vecs):
    nxt = pl.BlockSpec((IMAGE, D), lambda b, *_: (lax.rem(b + 1, TILES), 0))
    return pl.pallas_call(
        attend_kernel,
        grid_spec=pltpu.PrefetchScalarGridSpec(
            num_scalar_prefetch=1, grid=(TILES,),
            in_specs=[rows(D), nxt, rows(D), nxt, whole((D, 3 * D)), whole((1, TOTAL))],
            out_specs=[rows(D), rows(D), rows(D), rows(3 * D), rows(D), rows(128)],
            scratch_shapes=[pltpu.VMEM((2 * IMAGE + 8, D), f32)]),
        out_shape=[jax.ShapeDtypeStruct((LENGTH, D), bf16)] * 3
        + [jax.ShapeDtypeStruct((LENGTH, 3 * D), bf16), jax.ShapeDtypeStruct((LENGTH, D), bf16),
           jax.ShapeDtypeStruct((LENGTH, 128), f32)],
        compiler_params=params(), name="attend",
    )(shift, tokens, tokens, cot, cot, w, vecs)


def gelu_pair(v):
    half = 0.5 * (1.0 + lax.erf(v * 0.7071067811865476))
    slope = jnp.exp2(v * v * (-0.5 * LOG2E)) * 0.3989422804014327
    return v * half, half + v * slope


def widen_kernel(x, att, wo, wu, vecs, after_out, n_out, hid_out, gp_out):
    after = x[...].astype(f32) + dot(att[...], wo[...], NN) + vec(vecs, "bo")
    after_out[...] = after
    xhat, _ = standard(after)
    normed = (xhat * vec(vecs, "g2") + vec(vecs, "b2")).astype(bf16)
    n_out[...] = normed
    for c in range(0, 4 * D, D):
        pre = dot(normed, wu[:, c:c + D], NN) + vec(vecs, "bu", c, D)
        value, slope = gelu_pair(pre)
        hid_out[:, c:c + D] = value.astype(bf16)
        gp_out[:, c:c + D] = slope.astype(bf16)


def widen(x, att, wo, wu, vecs):
    ff = wu.shape[1]
    return pl.pallas_call(
        widen_kernel, grid=(TILES,),
        in_specs=[rows(D), rows(D), whole((D, D)), whole((D, ff)), whole((1, TOTAL))],
        out_specs=[rows(D), rows(D), rows(ff), rows(ff)],
        out_shape=[jax.ShapeDtypeStruct((LENGTH, D), f32), jax.ShapeDtypeStruct((LENGTH, D), bf16),
                   jax.ShapeDtypeStruct((LENGTH, ff), bf16), jax.ShapeDtypeStruct((LENGTH, ff), bf16)],
        compiler_params=params(), name="widen",
    )(x, att, wo, wu, vecs)


def place(scratch, value, shift):
    near = aligned(shift)
    first = shift - near
    at = pl.multiple_of(pl.program_id(0) * IMAGE + near, 8)
    moved = pltpu.roll(jnp.concatenate([value, jnp.zeros((8, D), f32)]), first, 0)
    row = lax.broadcasted_iota(jnp.int32, (8, 1), 0)
    scratch[pl.ds(at, 8), :] = jnp.where(row < first, scratch[pl.ds(at, 8), :], moved[:8])
    scratch[pl.ds(pl.multiple_of(at + 8, 8), IMAGE), :] = moved[8:]


def wrapped(scratch, shift):
    row = lax.broadcasted_iota(jnp.int32, (IMAGE, 1), 0)
    return jnp.where(row < shift, scratch[LENGTH:LENGTH + IMAGE], scratch[:IMAGE])


def narrow_kernel(shift_ref, hid, gp, after, cot, wd, vecs, out, pre_out, bu_out, bd_out, scratch):
    shift = shift_ref[0]
    value = after[...] + dot(hid[...], wd[...], NN) + vec(vecs, "bd")
    place(scratch, value, shift)
    upper = cot[...]
    add_up(bd_out, col_sum(upper.astype(f32)))
    ff = hid.shape[1]

    @pl.when(pl.program_id(0) == 0)
    def _():
        bu_out[...] = jnp.zeros_like(bu_out)

    for c in range(0, ff, D):
        grad = dot(upper, wd[c:c + D, :], NT) * gp[:, c:c + D].astype(f32)
        grad = grad.astype(bf16)
        pre_out[:, c:c + D] = grad
        bu_out[:, c:c + D] += col_sum(grad.astype(f32))

    @pl.when(pl.program_id(0) == TILES - 1)
    def _():
        out[IMAGE:] = scratch[IMAGE:LENGTH].astype(bf16)
        out[:IMAGE] = wrapped(scratch, shift).astype(bf16)


def narrow(shift, hid, gp, after, cot, wd, vecs):
    ff = wd.shape[0]
    return pl.pallas_call(
        narrow_kernel,
        grid_spec=pltpu.PrefetchScalarGridSpec(
            num_scalar_prefetch=1, grid=(TILES,),
            in_specs=[rows(ff), rows(ff), rows(D), rows(D), whole((ff, D)), whole((1, TOTAL))],
            out_specs=[kept((LENGTH, D)), rows(ff), kept((1, ff)), kept((1, D))],
            scratch_shapes=[pltpu.VMEM((LENGTH + IMAGE + 8, D), f32)]),
        out_shape=[jax.ShapeDtypeStruct((LENGTH, D), bf16), jax.ShapeDtypeStruct((LENGTH, ff), bf16),
                   jax.ShapeDtypeStruct((1, ff), f32), jax.ShapeDtypeStruct((1, D), f32)],
        compiler_params=params(), name="narrow",
    )(shift, hid, gp, after, cot, wd, vecs)


def back_kernel(shift_ref, pre, after, cot, qkv, lse, wu, wo, vecs,
                ag_out, pg_out, dqkv_out, g2_out, b2_out, bo_out, bqkv_out):
    block = pl.program_id(0)
    shift = shift_ref[0]
    dn = dot(pre[...], wu[...], NT)
    xhat, inverse = standard(after[...])
    add_up(g2_out, col_sum(dn * xhat))
    add_up(b2_out, col_sum(dn))
    after_grad = cot[...].astype(f32) + norm_back(dn, xhat, inverse, vec(vecs, "g2"))
    ag_out[...] = after_grad
    proj = after_grad.astype(bf16)
    pg_out[...] = proj
    add_up(bo_out, col_sum(proj.astype(f32)))
    upper_all = dot(proj, wo[...], NT).astype(bf16)
    same = same_image(block, shift)
    count = D // 128
    sums = [[None] * count for _ in range(3)]
    for head in range(HEADS):
        first, start, width = window(head)
        mask = lane_mask(first, start, width)
        q = qkv[:, start:start + width]
        k = qkv[:, D + start:D + start + width]
        v = qkv[:, 2 * D + start:2 * D + start + width]
        u = upper_all[:, start:start + width]
        q = jnp.where(mask, q, jnp.zeros_like(q))
        k = jnp.where(mask, k, jnp.zeros_like(k))
        u = jnp.where(mask, u, jnp.zeros_like(u))
        scores = dot(q, k, NT)
        probs = jnp.exp2(scores * SCALE2 - lse[:, head:head + 1])
        probs = jnp.where(same, probs, 0.0)
        pgrad = dot(u, v, NT)
        centre = jnp.sum(probs * pgrad, axis=-1, keepdims=True)
        sg = (probs * (pgrad - centre)).astype(bf16)
        parts = (dot(sg, k, NN), dot(sg, q, TN), dot(probs.astype(bf16), u, TN))
        for which in range(3):
            for t in range(width // 128):
                at = start // 128 + t
                piece = parts[which][:, 128 * t:128 * t + 128]
                old = sums[which][at]
                sums[which][at] = piece if old is None else old + piece
    for which in range(3):
        for t in range(count):
            value = sums[which][t]
            if which < 2:
                value = value * HEAD_DIM ** (-0.5)
            dqkv_out[:, which * D + 128 * t:which * D + 128 * t + 128] = value.astype(bf16)
    add_up(bqkv_out, col_sum(dqkv_out[...].astype(f32)))


def back(shift, pre, after, cot, qkv, lse, wu, wo, vecs):
    ff = wu.shape[1]
    row = jax.ShapeDtypeStruct((1, D), f32)
    return pl.pallas_call(
        back_kernel,
        grid_spec=pltpu.PrefetchScalarGridSpec(
            num_scalar_prefetch=1, grid=(TILES,),
            in_specs=[rows(ff), rows(D), rows(D), rows(3 * D), rows(128), whole((D, ff)),
                      whole((D, D)), whole((1, TOTAL))],
            out_specs=[rows(D), rows(D), rows(3 * D), kept((1, D)), kept((1, D)), kept((1, D)),
                       kept((1, 3 * D))]),
        out_shape=[jax.ShapeDtypeStruct((LENGTH, D), f32), jax.ShapeDtypeStruct((LENGTH, D), bf16),
                   jax.ShapeDtypeStruct((LENGTH, 3 * D), bf16), row, row, row,
                   jax.ShapeDtypeStruct((1, 3 * D), f32)],
        compiler_params=params(), name="back",
    )(shift, pre, after, cot, qkv, lse, wu, wo, vecs)


def entry_kernel(shift_ref, dqkv, x, ag, w, vecs, tg_out, g1_out, b1_out, scratch):
    shift = shift_ref[0]
    dn = dot(dqkv[...], w[...], NT)
    xhat, inverse = standard(x[...].astype(f32))
    add_up(g1_out, col_sum(dn * xhat))
    add_up(b1_out, col_sum(dn))
    place(scratch, ag[...] + norm_back(dn, xhat, inverse, vec(vecs, "g1")), shift)

    @pl.when(pl.program_id(0) == TILES - 1)
    def _():
        tg_out[IMAGE:] = scratch[IMAGE:LENGTH]
        tg_out[:IMAGE] = wrapped(scratch, shift)


def entry(shift, dqkv, x, ag, w, vecs):
    row = jax.ShapeDtypeStruct((1, D), f32)
    return pl.pallas_call(
        entry_kernel,
        grid_spec=pltpu.PrefetchScalarGridSpec(
            num_scalar_prefetch=1, grid=(TILES,),
            in_specs=[rows(3 * D), rows(D), rows(D), whole((D, 3 * D)), whole((1, TOTAL))],
            out_specs=[kept((LENGTH, D)), kept((1, D)), kept((1, D))],
            scratch_shapes=[pltpu.VMEM((LENGTH + IMAGE + 8, D), f32)]),
        out_shape=[jax.ShapeDtypeStruct((LENGTH, D), f32), row, row],
        compiler_params=params(), name="entry",
    )(shift, dqkv, x, ag, w, vecs)


def product(left, right):
    return lax.dot_general(left, right, (TN, ((), ())), preferred_element_type=f32).astype(bf16)


def swap(value, flip, size):
    return lax.ppermute(value, "narrow", [(a, a ^ flip) for a in range(size)])


def both(first, second):
    return (first.astype(f32) + second.astype(f32)).astype(bf16)


def pick(value, index, axis):
    return lax.dynamic_index_in_dim(value, index, axis, keepdims=False)


def half(value, index):
    size = value.shape[1] // 2
    return lax.dynamic_slice_in_dim(value, index * size, size, 1)


def reduced(left, right, wide):
    place_n = lax.axis_index("narrow")
    core, side = place_n % 2, place_n // 2
    sent = product(left, half(right, 1 - core))
    arrived = swap(sent, 1, 4)
    own = product(left, half(right, core))
    cut = (wide, 2, own.shape[0] // (2 * wide), own.shape[1])
    own, arrived = own.reshape(cut), arrived.reshape(cut)
    moving = both(pick(own, 1 - side, 1), pick(arrived, 1 - side, 1))
    met = swap(moving, 2, 4)
    total = pick(own, side, 1).astype(f32) + pick(arrived, side, 1).astype(f32) + met.astype(f32)
    parts = lax.all_to_all(total.astype(bf16), "wide", split_axis=0, concat_axis=0, tiled=True)
    mine = jnp.sum(parts.astype(f32), axis=0).astype(bf16)
    every = lax.all_gather(mine, "narrow", axis=0, tiled=False)
    every = every.reshape(2, 2, cut[2], cut[3]).transpose(0, 2, 1, 3)
    return every.reshape(2 * cut[2], 2 * cut[3]).astype(f32)


def shards(wide, tokens, segment_ids, cotangent, ln1_gain, ln1_bias, qkv_weight, qv_bias,
           out_weight, out_bias, ln2_gain, ln2_bias, up_weight, up_bias, down_weight, down_bias):
    def gathered(value):
        return lax.all_gather(value, "wide", axis=0, tiled=True)

    small = jnp.concatenate([ln1_gain, ln1_bias, qv_bias, out_bias, ln2_gain, ln2_bias, up_bias, down_bias])
    small = lax.all_gather(small, "wide", axis=0, tiled=False).astype(f32)
    flat = []
    at = 0
    for value in (ln1_gain, ln1_bias, qv_bias, out_bias, ln2_gain, ln2_bias, up_bias, down_bias):
        flat.append(small[:, at:at + value.shape[0]].reshape(-1))
        at += value.shape[0]
    flat[2:3] = [flat[2][:D], jnp.zeros((D,), f32), flat[2][D:]]
    vecs = jnp.concatenate(flat).reshape(1, TOTAL)
    shift = jnp.sum((segment_ids == 0).astype(jnp.int32)).reshape(1)
    wq = gathered(qkv_weight)
    wo = gathered(out_weight)
    wu = gathered(up_weight)
    wd = gathered(down_weight)
    x, cot, first, qkv, att, lse = attend(shift, tokens, cotangent, wq, vecs)
    after, second, hid, gp = widen(x, att, wo, wu, vecs)
    down_grad = reduced(hid, cot, wide)
    out, pre, gbu, gbd = narrow(shift, hid, gp, after, cot, wd, vecs)
    up_grad = reduced(second, pre, wide)
    ag, proj, dqkv, gg2, gb2, gbo, gbq = back(shift, pre, after, cot, qkv, lse, wu, wo, vecs)
    out_grad = reduced(att, proj, wide)
    qkv_grad = reduced(first, dqkv, wide)
    tokens_grad, gg1, gb1 = entry(shift, dqkv, x, ag, wq, vecs)
    sums = jnp.concatenate([gg1, gb1, gbq[:, :D], gbq[:, 2 * D:], gbo, gg2, gb2, gbu, gbd], axis=1)[0]
    sums = lax.psum(sums, ("wide", "narrow"))
    index = lax.axis_index("wide")
    grads = []
    at = 0
    for value in (ln1_gain, ln1_bias, qv_bias, out_bias, ln2_gain, ln2_bias, up_bias, down_bias):
        size = value.shape[0]
        grads.append(lax.dynamic_slice_in_dim(sums, at + index * size, size))
        at += size * wide
    g1, b1, bq, bo, g2, b2, bu, bd = grads
    return (out, tokens_grad, g1, b1, qkv_grad, bq, out_grad, bo, g2, b2, up_grad, bu, down_grad, bd)


def solution(mesh):
    wide = mesh.shape["wide"]
    token = P(("wide", "narrow"), None)
    row, flat = P("wide", None), P("wide")
    ins = (token, P(("wide", "narrow")), token, flat, flat, row, flat, row, flat, flat, flat, row, flat, row, flat)
    outs = (token, token, flat, flat, row, flat, row, flat, flat, flat, row, flat, row, flat)
    return jax.shard_map(functools.partial(shards, wide), mesh=mesh, in_specs=ins, out_specs=outs, check_vma=False)
```

time: 1020 us -> 579 us (0.57)
  matrix products: 305 us -> 28.8 us
  waiting for transfers between devices: 420 us -> 239 us
  Pallas kernels: 0 us -> 122 us
  other arithmetic: 105 us -> 18.3 us
  local copies, waits for them, and re-layouts: 48.5 us -> 15.8 us
  starting transfers between devices: 0.36 us -> 23.1 us
    reduce_scatter x4 -> x0, waiting for transfers between devices: 352 us -> none  [the longest x1 163 us: shards(): lax.psum_scatter(up_weight_part, 'wide', scatter_dimension=0, tiled=True)]
    dot_general x68 -> x8, matrix products: 305 us -> 28.8 us  [product(): lax.dot_general(left, right, (TN, ((), ())), preferred_element_type=f32)]
    all_gather x4, waiting for transfers between devices: 27.2 us -> 193 us  [gathered(): return lax.all_gather(value, 'wide', axis=0, tiled=True)]
    pallas_call x0 -> x5, Pallas kernels: none -> 122 us  [the longest x1 45.6 us: back(): pl.pallas_call(back_kernel, grid_spec=pltpu.PrefetchScalarGridSpec(num_sc...]
    unnamed x2 -> x0, blocking collectives: 76.5 us -> none
    ppermute x0 -> x8, waiting for transfers between devices: none -> 42.8 us  [swap(): return lax.ppermute(value, 'narrow', [(a, a ^ flip) for a in range(size)])]
    psum x1, blocking collectives: 5.73 us -> 46.4 us  [shards(): sums = lax.psum(sums, ('wide', 'narrow'))]
    psum x1 -> x0, waiting for transfers between devices: 37.6 us -> none  [shards(): lax.psum(wide_mix.astype(jnp.bfloat16), 'narrow').astype(jnp.float32)]
  transfers between devices with their start and end apart: 9 -> 16, of which waited for: 5 -> 8; matrix products, arithmetic and copies ran while one was open for 40% -> 10% of each run, Pallas kernels for 0% -> 10%
where the time goes in v1:
time: 579 us; the launch traced here: 570 us
  waiting for transfers between devices  239 us (41%)
  Pallas kernels  122 us (21%)
  blocking collectives  108 us (19%)
  matrix products  28.8 us (5%)
  starting transfers between devices  23.1 us (4%)
  other arithmetic  18.3 us (3%)
  local copies, waits for them, and re-layouts  15.8 us (3%)
  between operations  14.9 us (3%)
    all_gather x4, waiting for transfers between devices, gathered(): return lax.all_gather(value, 'wide', axis=0, tiled=True)  193 us
    psum x1, blocking collectives, shards(): sums = lax.psum(sums, ('wide', 'narrow'))  46.4 us
    pallas_call x1, Pallas kernels, back(): pl.pallas_call(back_kernel, grid_spec=pltpu.PrefetchScalarGridSpec(num_sc...  45.6 us
    ppermute x8, waiting for transfers between devices, swap(): return lax.ppermute(value, 'narrow', [(a, a ^ flip) for a in range(size)])  42.8 us
    all_gather x1, blocking collectives, shards(): small = lax.all_gather(small, 'wide', axis=0, tiled=False).astype(f32)  32.9 us
    dot_general x8, matrix products, product(): lax.dot_general(left, right, (TN, ((), ())), preferred_element_type=f32)  28.8 us
    all_gather x4, blocking collectives, reduced(): every = lax.all_gather(mine, 'narrow', axis=0, tiled=False)  28.4 us
    pallas_call x1, Pallas kernels, attend(): pl.pallas_call(attend_kernel, grid_spec=pltpu.PrefetchScalarGridSpec(num_...  24.4 us
  transfers between devices with their start and end apart: 16, of which 8 were waited for; matrix products, arithmetic and copies ran while one was open for 10% of the time, Pallas kernels for 10%

profile of v1, /device:TPU:0, one launch (start us, length us, event | category | flops | bytes accessed | tf_op | source)
XLA Modules:
  0.0 569.9 jit_solution(1996582459436028587)
XLA Ops:
  10.3 32.9 %all-gather.5 = bf16[8,1,1152]{2,1,0:T(2,128)(2,1)S(1)} all-gather(bf16[1,1,1152]{2,1,0:T(2,128)(2,1)S(1)} %reshape.173), channel_id=2, replica_groups=mesh['wide'=8,'narrow'=4] {'wide'}, dimensions={0}, use_global_device_ids=true | all-gather | bytes 20736 | tf_op jit(solution)/shard_map/all_gather | solution.py:403
  45.4 32.4 %all-gather.11.cloned.1.call-done.w = bf16[768,2304]{1,0:T(8,128)(2,1)} async-done(((bf16[96,2304]{1,0:T(8,128)(2,1)}), bf16[768,2304]{1,0:T(8,128)(2,1)}) %all-gather.11.cloned.1.call-update) | async-done | bytes 3538960 | tf_op jit(solution)/shard_map/all_gather | solution.py:400
  77.8 24.4 %attend.1 = (bf16[1024,768]{1,0:T(8,128)(2,1)}, bf16[1024,768]{1,0:T(8,128)(2,1)}, bf16[1024,768]{1,0:T(8,128)(2,1)}, bf16[1024,2304]{1,0:T(8,128)(2,1)}, bf16[1...) custom-call(s32[1]{0:T(128)} %bitcast.shift_ref, bf16[1024,768]{1,0:T(8,128)(2,1)} %xb.1, bf16[1024,768]{1,0:T(8,128)(2,1)} %xb.1, ...), custom_call_target="tpu_custom_call" | custom-call | tf_op jit(solution)/shard_map/attend/pallas_call | solution.py:164
  102.2 17.7 %all-gather.13.cloned.1.call-done.wo = bf16[768,768]{1,0:T(8,128)(2,1)} async-done(((bf16[96,768]{1,0:T(8,128)(2,1)}), bf16[768,768]{1,0:T(8,128)(2,1)}) %all-gather.13.cloned.1.call-update) | async-done | bytes 1179664 | tf_op jit(solution)/shard_map/all_gather | solution.py:400
  119.9 80.2 %all-gather.15.cloned.1.call-done.wu = bf16[768,3072]{1,0:T(8,128)(2,1)} async-done(((bf16[96,3072]{1,0:T(8,128)(2,1)}), bf16[768,3072]{1,0:T(8,128)(2,1)}) %all-gather.15.cloned.1.call-update) | async-done | bytes 4718608 | tf_op jit(solution)/shard_map/all_gather | solution.py:400
  200.1 16.8 %widen.1 = (f32[1024,768]{1,0:T(8,128)}, bf16[1024,768]{1,0:T(8,128)(2,1)}, bf16[1024,3072]{1,0:T(8,128)(2,1)}, bf16[1024,3072]{1,0:T(8,128)(2,1)}) custom-call(bf16[1024,768]{1,0:T(8,128)(2,1)} %get-tuple-element.38.x, bf16[1024,768]{1,0:T(8,128)(2,1)} %get-tuple-element.39.att, bf16[768,768]{1,0:T(8,128)(2,1)} %all-gather.13.cloned.1.call-done.wo, ...), custom_call_target="tpu_custom_call" | custom-call | tf_op jit(solution)/shard_map/widen/pallas_call | solution.py:199
  217.0 62.9 %all-gather.17.cloned.1.call-done.wd = bf16[3072,768]{1,0:T(8,128)(2,1)} async-done(((bf16[384,768]{1,0:T(8,128)(2,1)}), bf16[3072,768]{1,0:T(8,128)(2,1)}) %all-gather.17.cloned.1.call-update) | async-done | bytes 4718608 | tf_op jit(solution)/shard_map/all_gather | solution.py:400
  279.9 22.1 %narrow.1 = (bf16[1024,768]{1,0:T(8,128)(2,1)}, bf16[1024,3072]{1,0:T(8,128)(2,1)}, f32[1,3072]{1,0:T(1,128)}, f32[1,768]{1,0:T(1,128)}) custom-call(s32[1]{0:T(128)} %bitcast.shift_ref, bf16[1024,3072]{1,0:T(8,128)(2,1)} %get-tuple-element.40.hid, bf16[1024,3072]{1,0:T(8,128)(2,1)} %get-tuple-element.41.gp, f32[1024,768]{1,0:T(8,128)} %get-tuple-element.42.after, ...), custom_call_target="tpu_custom_call" | custom-call | tf_op jit(solution)/shard_map/narrow/pallas_call | solution.py:250
  302.0 45.6 %back.1 = (f32[1024,768]{1,0:T(8,128)}, bf16[1024,768]{1,0:T(8,128)(2,1)}, bf16[1024,2304]{1,0:T(8,128)(2,1)}, f32[1,768]{1,0:T(1,128)}, f32[1,768]{1,0:T(1,128)}, /*index=5*/f32[1,768]{1,0:T(1,128)}, f32[1,2304]{1,0:T(1,128)}) custom-call(s32[1]{0:T(128)} %bitcast.shift_ref, bf16[1024,3072]{1,0:T(8,128)(2,1)} %get-tuple-element.45.pre, ...), custom_call_target="tpu_custom_call" | custom-call | tf_op jit(solution)/shard_map/back/pallas_call | solution.py:315
  347.7 4.1 convolution_convert_fusion.4
  351.9 2.3 convolution_convert_fusion.6
  354.7 4.2 convolution_convert_fusion.2
  359.0 4.8 convolution_convert_fusion
  364.2 1.0 convolution_convert_fusion.7
  365.3 2.2 convolution_convert_fusion.5
  367.6 1.5 collective-permute-start.3
  370.2 4.0 convolution_convert_fusion.3
  374.2 3.4 collective-permute-done.3
  378.4 3.4 all-to-all-start.1
  381.9 3.1 fusion.7
  385.0 1.5 collective-permute-start.5
  386.4 10.2 %collective-permute-done.1 = bf16[8,48,1152]{2,1,0:T(8,128)(2,1)} collective-permute-done((bf16[8,48,1152]{2,1,0:T(8,128)(2,1)S(1)}, bf16[8,48,1152]{2,1,0:T(8,128)(2,1)}, u32[]{:S(2)}, u32[]{:S(2)}) %collective-permute-start.1) | collective-permute-done | bytes 884768 | tf_op jit(solution)/shard_map/ppermute | solution.py:363
  396.6 2.4 fusion.6
  399.0 3.6 all-to-all-start
  402.6 18.4 %collective-permute-done.5 = bf16[8,48,1536]{2,1,0:T(8,128)(2,1)} collective-permute-done((bf16[8,48,1536]{2,1,0:T(8,128)(2,1)}, bf16[8,48,1536]{2,1,0:T(8,128)(2,1)}, u32[]{:S(2)}, u32[]{:S(2)}) %collective-permute-start.5) | collective-permute-done | bytes 1179680 | tf_op jit(solution)/shard_map/ppermute | solution.py:363
  421.0 3.4 fusion.3
  424.4 0.9 copy-done.2
  425.4 3.8 all-to-all-start.2
  429.2 6.3 %convolution_convert_fusion.1 = bf16[3072,384]{1,0:T(8,128)(2,1)S(1)} fusion(bf16[1024,3072]{1,0:T(8,128)(2,1)} %get-tuple-element.40.hid, bf16[1024,768]{1,0:T(8,128)(2,1)S(1)} %copy-done, s32[]{:T(128)S(6)} %select_n.97), kind=kOutput, calls=%fused_computation.1 | convolution fusion | flops 2417098752 | bytes 9437188 | tf_op jit(solution)/shard_map/dot_general | solution.py:359
  435.5 3.4 fusion.8
  438.9 1.5 collective-permute-start.7
  440.4 13.6 %entry.1 = (f32[1024,768]{1,0:T(8,128)}, f32[1,768]{1,0:T(1,128)}, f32[1,768]{1,0:T(1,128)}) custom-call(s32[1]{0:T(128)} %bitcast.shift_ref, bf16[1024,2304]{1,0:T(8,128)(2,1)} %get-tuple-element.48.dqkv, bf16[1024,768]{1,0:T(8,128)(2,1)} %get-tuple-element.38.x, f32[1024,768]{1,0:T(8,128)} %get-tuple-element.49.ag, ...), custom_call_target="tpu_custom_call" | custom-call | tf_op jit(solution)/shard_map/entry/pallas_call | solution.py:346
  455.4 10.8 %collective-permute-done.7 = bf16[8,192,384]{2,1,0:T(8,128)(2,1)S(1)} collective-permute-done((bf16[8,192,384]{2,1,0:T(8,128)(2,1)}, bf16[8,192,384]{2,1,0:T(8,128)(2,1)S(1)}, u32[]{:S(2)}, u32[]{:S(2)}) %collective-permute-start.7) | collective-permute-done | bytes 1179680 | tf_op jit(solution)/shard_map/ppermute | solution.py:363
  466.2 2.8 fusion.2
  469.0 5.8 %all-to-all-start.3 = ((bf16[8,192,384]{2,1,0:T(8,128)(2,1)}), bf16[8,192,384]{2,1,0:T(8,128)(2,1)S(1)}, u32[]{:S(2)}, u32[]{:S(2)}) async-start(bf16[8,192,384]{2,1,0:T(8,128)(2,1)} %fusion.2), calls=%async_computation.3 | async-start | bytes 2359296 | tf_op jit(solution)/shard_map/all_to_all | solution.py:390
  476.0 46.4 %psum.7 = f32[9216]{0:T(1024)} all-reduce(f32[9216]{0:T(1024)} %bitcast.120), channel_id=1, replica_groups=mesh['wide'=8,'narrow'=4] {'wide','narrow'}, use_global_device_ids=true, to_apply=%region_1.2 | all-reduce | flops 9216 | bytes 73728 | tf_op jit(solution)/shard_map/psum | solution.py:426
  522.5 1.3 dynamic_slice.108
  523.8 1.3 dynamic_slice.124
  525.2 1.4 fusion.24
  527.2 6.1 %all-gather.2 = bf16[192,384]{1,0:T(8,128)(2,1)S(1)} all-gather(bf16[48,384]{1,0:T(8,128)(2,1)} %reduce_sum.59), channel_id=4, replica_groups=mesh['wide'=8,'narrow'=4] {'narrow'}, dimensions={0}, use_global_device_ids=true | all-gather | bytes 184320 | tf_op jit(solution)/shard_map/all_gather | solution.py:392
  534.4 7.1 %all-gather.1 = bf16[192,1152]{1,0:T(8,128)(2,1)S(1)} all-gather(bf16[48,1152]{1,0:T(8,128)(2,1)S(1)} %reduce_sum.58), channel_id=3, replica_groups=mesh['wide'=8,'narrow'=4] {'narrow'}, dimensions={0}, use_global_device_ids=true | all-gather | bytes 552960 | tf_op jit(solution)/shard_map/all_gather | solution.py:392
  542.0 1.0 copy.78
  543.1 7.6 %all-gather.3 = bf16[192,1536]{1,0:T(8,128)(2,1)S(1)} all-gather(bf16[48,1536]{1,0:T(8,128)(2,1)S(1)} %reduce_sum.60), channel_id=5, replica_groups=mesh['wide'=8,'narrow'=4] {'narrow'}, dimensions={0}, use_global_device_ids=true | all-gather | bytes 737280 | tf_op jit(solution)/shard_map/all_gather | solution.py:392
  550.9 0.9 copy.65
  551.8 1.2 copy.80
  553.2 7.6 %all-gather.4 = bf16[768,384]{1,0:T(8,128)(2,1)S(1)} all-gather(bf16[192,384]{1,0:T(8,128)(2,1)S(1)} %reduce_sum.61), channel_id=6, replica_groups=mesh['wide'=8,'narrow'=4] {'narrow'}, dimensions={0}, use_global_device_ids=true | all-gather | bytes 737280 | tf_op jit(solution)/shard_map/all_gather | solution.py:392
  560.9 0.9 copy.68
  561.8 1.1 copy.81
  (141 shorter events, 13.5 us)
Async XLA Ops:
  7.2 2.9 copy-start.20
  7.2 2.9 copy-start.21
  7.2 2.9 copy-start.22
  7.2 2.9 copy-start.23
  7.2 2.9 copy-start.24
  7.2 2.9 copy-start.25
  7.2 2.9 copy-start.19
  7.3 2.9 copy-start.26
  7.3 37.5 %copy-start.14 = (s32[1024]{0:T(1024)S(1)}, s32[1024]{0:T(1024)}, u32[]{:S(2)}) copy-start(s32[1024]{0:T(1024)} %param.16) | copy-start | bytes 12292
  7.3 70.6 %all-gather.11.cloned.1.call-start = ((), (), s32[]{:S(2)}) async-start(), calls=%async_computation.4 | async-start | bytes 3981312 | tf_op jit(solution)/shard_map/all_gather | solution.py:400
  8.0 111.9 %all-gather.13.cloned.1.call-start = ((), (), s32[]{:S(2)}) async-start(), calls=%async_computation.5 | async-start | bytes 1327104 | tf_op jit(solution)/shard_map/all_gather | solution.py:400
  8.8 191.4 %all-gather.15.cloned.1.call-start = ((), (), s32[]{:S(2)}) async-start(), calls=%async_computation.6 | async-start | bytes 5308416 | tf_op jit(solution)/shard_map/all_gather | solution.py:400
  9.5 270.4 %all-gather.17.cloned.1.call-start = ((), (), s32[]{:S(2)}) async-start(), calls=%async_computation.7 | async-start | bytes 5308416 | tf_op jit(solution)/shard_map/all_gather | solution.py:400
  302.0 45.6 %copy-start.28 = (bf16[1024,768]{1,0:T(8,128)(2,1)S(1)}, bf16[1024,768]{1,0:T(8,128)(2,1)}, u32[]{:S(2)}) copy-start(bf16[1024,768]{1,0:T(8,128)(2,1)} %get-tuple-element.59) | copy-start | bytes 4718596
  302.0 49.8 %copy-start.10 = (bf16[1024,768]{1,0:T(8,128)(2,1)S(1)}, bf16[1024,768]{1,0:T(8,128)(2,1)}, u32[]{:S(2)}) copy-start(bf16[1024,768]{1,0:T(8,128)(2,1)} %get-tuple-element.39.att) | copy-start | bytes 4718596
  347.7 7.0 %copy-start.1 = (bf16[1024,3072]{1,0:T(8,128)(2,1)S(1)}, bf16[1024,3072]{1,0:T(8,128)(2,1)}, u32[]{:S(2)}) copy-start(bf16[1024,3072]{1,0:T(8,128)(2,1)} %get-tuple-element.45.pre) | copy-start | bytes 18874372
  347.7 7.0 %copy-start.27 = (bf16[1024,768]{1,0:T(8,128)(2,1)S(1)}, bf16[1024,768]{1,0:T(8,128)(2,1)}, u32[]{:S(2)}) copy-start(bf16[1024,768]{1,0:T(8,128)(2,1)} %get-tuple-element.61) | copy-start | bytes 4718596
  351.8 17.4 %collective-permute-start = (bf16[768,1152]{1,0:T(8,128)(2,1)S(1)}, bf16[768,1152]{1,0:T(8,128)(2,1)S(1)}, u32[]{:S(2)}, u32[]{:S(2)}) collective-permute-start(bf16[768,1152]{1,0:T(8,128)(2,1)S(1)} %convolution_convert_fusion.4), channel_id=1, source_target_pairs={{0,1},{1,0},{2,3},{3,2},{4,5},{5,4},{6,7},{7,6},{8,9},{9,8},{10,11... | collective-permute-start | bytes 5308424 | tf_op jit(solution)/shard_map/ppermute | solution.py:363
  351.8 7.1 %slice-start = ((s8[6291456]{0:T(1024)(128)(4,1)}), s8[4194304]{0:T(1024)(128)(4,1)S(1)}, s32[]{:S(2)}) async-start(s8[6291456]{0:T(1024)(128)(4,1)} %bitcast.89), calls=%async_computation.8 | async-start | bytes 8388608
  354.2 13.4 %collective-permute-start.2 = (bf16[768,384]{1,0:T(8,128)(2,1)S(1)}, bf16[768,384]{1,0:T(8,128)(2,1)S(1)}, u32[]{:S(2)}, u32[]{:S(2)}) collective-permute-start(bf16[768,384]{1,0:T(8,128)(2,1)S(1)} %convolution_convert_fusion.6), channel_id=1, source_target_pairs={{0,1},{1,0},{2,3},{3,2},{4,5},{5,4},{6,7},{7,6},{8,9},{9,8},{10,11... | collective-permute-start | bytes 1769480 | tf_op jit(solution)/shard_map/ppermute | solution.py:363
  354.7 4.2 copy-start
  354.7 4.2 slice-start.1
  354.7 10.5 %slice-start.2 = ((s8[4718592]{0:T(1024)(128)(4,1)}), s8[4194304]{0:T(1024)(128)(4,1)S(1)}, s32[]{:S(2)}) async-start(s8[4718592]{0:T(1024)(128)(4,1)} %bitcast.91), calls=%async_computation.10 | async-start | bytes 8388608
  358.9 5.3 copy-start.29
  358.9 6.3 %slice-start.3 = ((s8[4718592]{0:T(1024)(128)(4,1)}), s8[524288]{0:T(1024)(128)(4,1)S(1)}, s32[]{:S(2)}) async-start(s8[4718592]{0:T(1024)(128)(4,1)} %bitcast.91), calls=%async_computation.11 | async-start | bytes 1048576
  358.9 22.9 %collective-permute-start.4 = (bf16[768,1536]{1,0:T(8,128)(2,1)}, bf16[768,1536]{1,0:T(8,128)(2,1)}, u32[]{:S(2)}, u32[]{:S(2)}) collective-permute-start(bf16[768,1536]{1,0:T(8,128)(2,1)} %convolution_convert_fusion.2), channel_id=1, source_target_pairs={{0,1},{1,0},{2,3},{3,2},{4,5},{5,4},{6,7},{7,6},{8,9},{9,8},{10,11... | collective-permute-start | bytes 7077896 | tf_op jit(solution)/shard_map/ppermute | solution.py:363
  363.7 71.7 %collective-permute-start.6 = (bf16[3072,384]{1,0:T(8,128)(2,1)}, bf16[3072,384]{1,0:T(8,128)(2,1)}, u32[]{:S(2)}, u32[]{:S(2)}) collective-permute-start(bf16[3072,384]{1,0:T(8,128)(2,1)} %convolution_convert_fusion), channel_id=1, source_target_pairs={{0,1},{1,0},{2,3},{3,2},{4,5},{5,4},{6,7},{7,6},{8,9},{9,8},{10,11... | collective-permute-start | bytes 7077896 | tf_op jit(solution)/shard_map/ppermute | solution.py:363
  367.6 9.9 %collective-permute-start.3 = (bf16[8,48,384]{2,1,0:T(8,128)(2,1)S(1)}, bf16[8,48,384]{2,1,0:T(8,128)(2,1)S(1)}, u32[]{:S(2)}, u32[]{:S(2)}) collective-permute-start(bf16[8,48,384]{2,1,0:T(8,128)(2,1)S(1)} %fusion.15), channel_id=1, source_target_pairs={{0,2},{1,3},{2,0},{3,1},{4,6},{5,7},{6,4},{7,5},{8,10},{9,11},{10,... | collective-permute-start | bytes 884744 | tf_op jit(solution)/shard_map/ppermute | solution.py:363
  369.2 5.0 copy-start.6
  369.4 27.2 %collective-permute-start.1 = (bf16[8,48,1152]{2,1,0:T(8,128)(2,1)S(1)}, bf16[8,48,1152]{2,1,0:T(8,128)(2,1)}, u32[]{:S(2)}, u32[]{:S(2)}) collective-permute-start(bf16[8,48,1152]{2,1,0:T(8,128)(2,1)S(1)} %fusion.9), channel_id=1, source_target_pairs={{0,2},{1,3},{2,0},{3,1},{4,6},{5,7},{6,4},{7,5},{8,10},{9,11},{10,... | collective-permute-start | bytes 2654216 | tf_op jit(solution)/shard_map/ppermute | solution.py:363
  378.4 20.6 %all-to-all-start.1 = ((bf16[8,48,384]{2,1,0:T(8,128)(2,1)}), bf16[8,48,384]{2,1,0:T(8,128)(2,1)S(1)}, u32[]{:S(2)}, u32[]{:S(2)}) async-start(bf16[8,48,384]{2,1,0:T(8,128)(2,1)} %fusion.14), calls=%async_computation.1 | async-start | bytes 589824 | tf_op jit(solution)/shard_map/all_to_all | solution.py:390
  381.8 14.8 %copy-start.7 = (bf16[768,1152]{1,0:T(8,128)(2,1)S(1)}, bf16[768,1152]{1,0:T(8,128)(2,1)}, u32[]{:S(2)}) copy-start(bf16[768,1152]{1,0:T(8,128)(2,1)} %copy-done.6) | copy-start | bytes 5308420
  381.9 14.8 %copy-start.9 = (bf16[768,1152]{1,0:T(8,128)(2,1)S(1)}, bf16[768,1152]{1,0:T(8,128)(2,1)}, u32[]{:S(2)}) copy-start(bf16[768,1152]{1,0:T(8,128)(2,1)} %copy-done.8) | copy-start | bytes 5308420
  385.0 36.0 %collective-permute-start.5 = (bf16[8,48,1536]{2,1,0:T(8,128)(2,1)}, bf16[8,48,1536]{2,1,0:T(8,128)(2,1)}, u32[]{:S(2)}, u32[]{:S(2)}) collective-permute-start(bf16[8,48,1536]{2,1,0:T(8,128)(2,1)} %fusion.7), channel_id=1, source_target_pairs={{0,2},{1,3},{2,0},{3,1},{4,6},{5,7},{6,4},{7,5},{8,10},{9,11},{10,... | collective-permute-start | bytes 3538952 | tf_op jit(solution)/shard_map/ppermute | solution.py:363
  399.0 25.4 %all-to-all-start = ((bf16[8,48,1152]{2,1,0:T(8,128)(2,1)}), bf16[8,48,1152]{2,1,0:T(8,128)(2,1)S(1)}, u32[]{:S(2)}, u32[]{:S(2)}) async-start(bf16[8,48,1152]{2,1,0:T(8,128)(2,1)} %fusion.6), calls=%async_computation | async-start | bytes 1769472 | tf_op jit(solution)/shard_map/all_to_all | solution.py:390
  425.4 43.6 %all-to-all-start.2 = ((bf16[8,48,1536]{2,1,0:T(8,128)(2,1)}), bf16[8,48,1536]{2,1,0:T(8,128)(2,1)S(1)}, u32[]{:S(2)}, u32[]{:S(2)}) async-start(bf16[8,48,1536]{2,1,0:T(8,128)(2,1)} %fusion.3), calls=%async_computation.2 | async-start | bytes 2359296 | tf_op jit(solution)/shard_map/all_to_all | solution.py:390
  435.4 3.5 copy-start.4
  438.9 27.3 %collective-permute-start.7 = (bf16[8,192,384]{2,1,0:T(8,128)(2,1)}, bf16[8,192,384]{2,1,0:T(8,128)(2,1)S(1)}, u32[]{:S(2)}, u32[]{:S(2)}) collective-permute-start(bf16[8,192,384]{2,1,0:T(8,128)(2,1)} %fusion.8), channel_id=1, source_target_pairs={{0,2},{1,3},{2,0},{3,1},{4,6},{5,7},{6,4},{7,5},{8,10},{9,11},{10,... | collective-permute-start | bytes 3538952 | tf_op jit(solution)/shard_map/ppermute | solution.py:363
  440.4 14.9 %copy-start.13 = (f32[1,2304]{1,0:T(1,128)S(1)}, f32[1,2304]{1,0:T(1,128)}, u32[]{:S(2)}) copy-start(f32[1,2304]{1,0:T(1,128)} %get-tuple-element.53) | copy-start | bytes 27652
  440.4 15.0 %copy-start.18 = (f32[1,768]{1,0:T(1,128)S(1)}, f32[1,768]{1,0:T(1,128)}, u32[]{:S(2)}) copy-start(f32[1,768]{1,0:T(1,128)} %get-tuple-element.54) | copy-start | bytes 9220
  440.4 15.0 %copy-start.17 = (f32[1,768]{1,0:T(1,128)S(1)}, f32[1,768]{1,0:T(1,128)}, u32[]{:S(2)}) copy-start(f32[1,768]{1,0:T(1,128)} %get-tuple-element.55) | copy-start | bytes 9220
  440.4 15.0 %copy-start.16 = (f32[1,768]{1,0:T(1,128)S(1)}, f32[1,768]{1,0:T(1,128)}, u32[]{:S(2)}) copy-start(f32[1,768]{1,0:T(1,128)} %get-tuple-element.56) | copy-start | bytes 9220
  440.4 25.8 %copy-start.5 = (bf16[3072,384]{1,0:T(8,128)(2,1)S(1)}, bf16[3072,384]{1,0:T(8,128)(2,1)}, u32[]{:S(2)}) copy-start(bf16[3072,384]{1,0:T(8,128)(2,1)} %copy-done.4) | copy-start | bytes 7077892
  455.4 10.8 %copy-start.11 = (f32[1,9216]{1,0:T(1,128)}, f32[1,9216]{1,0:T(1,128)S(1)}, u32[]{:S(2)}) copy-start(f32[1,9216]{1,0:T(1,128)S(1)} %constant_dynamic-update-slice_fusion.3) | copy-start | bytes 110596
  469.0 5.8 %copy-start.12 = (f32[1,3072]{1,0:T(1,128)S(1)}, f32[1,3072]{1,0:T(1,128)}, u32[]{:S(2)}) copy-start(f32[1,3072]{1,0:T(1,128)} %get-tuple-element.57) | copy-start | bytes 36868
  469.0 6.5 %copy-start.15 = (f32[1,768]{1,0:T(1,128)S(1)}, f32[1,768]{1,0:T(1,128)}, u32[]{:S(2)}) copy-start(f32[1,768]{1,0:T(1,128)} %get-tuple-element.58) | copy-start | bytes 9220
  469.0 65.3 %copy-start.3 = (bf16[8,48,1152]{2,1,0:T(8,128)(2,1)S(1)}, bf16[8,48,1152]{2,1,0:T(8,128)(2,1)}, u32[]{:S(2)}) copy-start(bf16[8,48,1152]{2,1,0:T(8,128)(2,1)} %copy-done.2) | copy-start | bytes 2654212
  469.0 84.0 %all-to-all-start.3 = ((bf16[8,192,384]{2,1,0:T(8,128)(2,1)}), bf16[8,192,384]{2,1,0:T(8,128)(2,1)S(1)}, u32[]{:S(2)}, u32[]{:S(2)}) async-start(bf16[8,192,384]{2,1,0:T(8,128)(2,1)} %fusion.2), calls=%async_computation.3 | async-start | bytes 2359296 | tf_op jit(solution)/shard_map/all_to_all | solution.py:390
  (2 other events, 2.8 us)
Sparse Core Ops, SparseCore 0:
  10.3 67.5 all-gather.10
  80.0 39.8 all-gather.12
  122.1 78.0 all-gather.14
  202.2 77.6 all-gather.16
